TPU v7x, 32 devices: a whole 2x2x4 slice. The times are simulated.
32 devices in a mesh: section: 4 (over z), ctx: 8 (over y, x, core).
Axes of the slice: x: 2, y: 2, z: 4, core: 2. Of those that a mesh axis runs over, the one named last changes fastest.
Arguments:
- stream: bfloat16 [1024, 2688], P('ctx'), may hold values from -6 to 6
- queries: bfloat16 [4, 1024, 2048], P('section', 'ctx'), may hold values from -51 to 51
- keys: bfloat16 [4, 1024, 1024], P('section', 'ctx'), may hold values from -4 to 4
- values: bfloat16 [4, 1024, 1024], P('section', 'ctx'), may hold values from -120 to 120
- out_weight: bfloat16 [4, 2048, 2688], P('section', 'ctx'), may hold values from -0.125 to 0.125
- gains: bfloat16 [4, 2688], P('section'), may hold values from 0.099609375 to 1.8984375
Outputs:
- layer_outputs: bfloat16 [4, 1024, 2688], P('section', 'ctx')
All inputs are finite; a program needn't handle non-finite values.
Results may differ from a plain program's by a relative error of at most 0.009.
Values may be sent and summed in bfloat16 or wider, within the bound.
A program may use at most 64 MiB of HBM per device.

v0:
```python
import math

import jax
import jax.numpy as jnp
from jax import lax
from jax.sharding import PartitionSpec as P

KEY_HEADS = 8
HEAD_WIDTH = 128
WINDOW_LENGTH = 1024
QUERY_SCALAR = 168
QUERY_PER_KEY = 2


norm_eps = 1e-06


def passed_along(block, axis, distance):
    devices = range(lax.axis_size(axis))
    route = [(i - distance, i) for i in devices if i - distance in devices]
    return lax.ppermute(block, axis, route)


def attend_block(query_matrix_rows, key_matrix_rows, value_matrix_rows, allowed, scale_factor):
    scores = (
        jnp.einsum(
            "qhgd,khd->hgqk", query_matrix_rows, key_matrix_rows, preferred_element_type=jnp.float32
        )
        * scale_factor
    )
    scores = jnp.where(allowed, scores, -jnp.inf)
    row_top = jnp.max(scores, axis=-1, keepdims=True)
    exponent = jnp.exp(scores - row_top)
    row_total = jnp.sum(exponent, axis=-1, keepdims=True)
    weights = exponent.astype(jnp.bfloat16)
    mixed_rows = jnp.einsum(
        "hgqk,khd->qhgd", weights, value_matrix_rows, preferred_element_type=jnp.float32
    )
    return mixed_rows / jnp.transpose(row_total, (2, 0, 1, 3))


def local(stream, queries, keys, values, out_weight, gains):
    tok_rows = stream.shape[0]
    span_rows = min(tok_rows, WINDOW_LENGTH)
    hop_count = WINDOW_LENGTH // span_rows
    own_tail = (keys[0, tok_rows - span_rows :], values[0, tok_rows - span_rows :])
    pieces = [
        passed_along((own_tail[0], own_tail[1]), "ctx", distance)
        for distance in range(hop_count, 0, -1)
    ]
    key_matrix_rows = jnp.concatenate([piece_pair[0] for piece_pair in pieces] + [keys[0]], axis=0)
    value_matrix_rows = jnp.concatenate(
        [piece_pair[1] for piece_pair in pieces] + [values[0]], axis=0
    )
    ctx_base = lax.axis_index("ctx") * tok_rows
    query_pos = ctx_base + jnp.arange(tok_rows, dtype=jnp.int32)
    key_pos = ctx_base - WINDOW_LENGTH + jnp.arange(WINDOW_LENGTH + tok_rows, dtype=jnp.int32)
    allowed = (
        (key_pos[None, :] >= 0)
        & (key_pos[None, :] <= query_pos[:, None])
        & (key_pos[None, :] > query_pos[:, None] - WINDOW_LENGTH)
    )
    scale_factor = QUERY_SCALAR ** (-0.5)
    heads_per_block = math.gcd(KEY_HEADS, 4)
    query_width = heads_per_block * QUERY_PER_KEY * HEAD_WIDTH
    key_width = heads_per_block * HEAD_WIDTH
    outputs_list = []
    for query_head_group in range(KEY_HEADS // heads_per_block):
        query_cols = queries[
            0, :, query_head_group * query_width : (query_head_group + 1) * query_width
        ].reshape(tok_rows, heads_per_block, QUERY_PER_KEY, HEAD_WIDTH)
        key_cols = key_matrix_rows[
            :, query_head_group * key_width : (query_head_group + 1) * key_width
        ].reshape(WINDOW_LENGTH + tok_rows, heads_per_block, HEAD_WIDTH)
        value_cols = value_matrix_rows[
            :, query_head_group * key_width : (query_head_group + 1) * key_width
        ].reshape(WINDOW_LENGTH + tok_rows, heads_per_block, HEAD_WIDTH)
        mixed_rows = attend_block(query_cols, key_cols, value_cols, allowed, scale_factor)
        outputs_list.append(mixed_rows.reshape(tok_rows, query_width))
    attended = jnp.concatenate(outputs_list, axis=1).astype(jnp.bfloat16)
    projected = jnp.dot(
        attended,
        lax.all_gather(out_weight[0], "ctx", axis=0, tiled=True),
        preferred_element_type=jnp.float32,
    )
    mean_square = jnp.mean(projected * projected, axis=-1, keepdims=True)
    branch = projected * lax.rsqrt(mean_square + norm_eps) * gains[0].astype(jnp.float32)
    section_index = lax.axis_index("section")
    section_count = lax.axis_size("section")
    running = jnp.where(
        section_index == 0, stream.astype(jnp.float32) + branch, jnp.zeros_like(branch)
    )
    for turn_index in range(section_count - 1):
        arrived = passed_along(running.astype(jnp.bfloat16), "section", 1).astype(running.dtype)
        running = jnp.where(section_index == turn_index + 1, arrived + branch, running)
    return running.astype(jnp.bfloat16)[None]


def solution(mesh):
    in_specs = (
        P("ctx", None),
        P("section", "ctx", None),
        P("section", "ctx", None),
        P("section", "ctx", None),
        P("section", "ctx", None),
        P("section", None),
    )
    out_specs = P("section", "ctx", None)
    return jax.shard_map(local, mesh=mesh, in_specs=in_specs, out_specs=out_specs, check_vma=False)
```

profile of v0, /device:TPU:12, one launch (start us, length us, event | category | flops | bytes accessed | tf_op | source)
XLA Modules:
  0.0 192.6 jit_solution(15729484851939583275)
XLA Ops:
  6.5 0.7 all-gather.3.cloned.1.call-update
  7.3 1.1 copy.12
  8.4 1.4 collective-permute-start.8
  9.7 1.4 collective-permute-start.9
  11.1 0.7 collective-permute-start
  11.8 0.7 collective-permute-start.1
  12.4 0.7 collective-permute-start.2
  13.2 0.9 compare_and_fusion
  14.2 0.2 copy.34
  14.4 0.8 copy.35
  15.2 0.0 collective-permute-done
  15.2 0.7 collective-permute-start.3
  15.9 0.0 collective-permute-done.1
  15.9 1.3 collective-permute-start.4
  17.3 14.6 %collective-permute-start.5 = (bf16[128,1024]{1,0:T(8,128)(2,1)S(1)}, bf16[128,1024]{1,0:T(8,128)(2,1)S(1)}, u32[]{:S(2)}, u32[]{:S(2)}) collective-permute-start(bf16[128,1024]{1,0:T(8,128)(2,1)S(1)} %bitcast.117), channel_id=1, source_target_pairs={{0,3},{1,4},{2,5},{3,6},{4,7},{8,11},{9,12},{10,13},{11,14},{12,15... | collective-permute-start | bytes 786440 | tf_op jit(solution)/shard_map/ppermute | solution.py:21
  31.9 0.0 collective-permute-done.3
  31.9 11.7 %collective-permute-start.6 = (bf16[128,1024]{1,0:T(8,128)(2,1)S(1)}, bf16[128,1024]{1,0:T(8,128)(2,1)S(1)}, u32[]{:S(2)}, u32[]{:S(2)}) collective-permute-start(bf16[128,1024]{1,0:T(8,128)(2,1)S(1)} %bitcast.118), channel_id=1, source_target_pairs={{0,2},{1,3},{2,4},{3,5},{4,6},{5,7},{8,10},{9,11},{10,12},{11,13},... | collective-permute-start | bytes 786440 | tf_op jit(solution)/shard_map/ppermute | solution.py:21
  43.6 10.3 %collective-permute-done.4 = bf16[128,1024]{1,0:T(8,128)(2,1)S(1)} collective-permute-done((bf16[128,1024]{1,0:T(8,128)(2,1)S(1)}, bf16[128,1024]{1,0:T(8,128)(2,1)S(1)}, u32[]{:S(2)}, u32[]{:S(2)}) %collective-permute-start.4) | collective-permute-done | bytes 262176 | tf_op jit(solution)/shard_map/ppermute | solution.py:21
  53.9 1.9 collective-permute-start.7
  55.9 0.0 collective-permute-done.5
  55.9 0.7 collective-permute-start.10
  56.6 0.0 collective-permute-done.6
  56.6 0.7 collective-permute-start.11
  57.3 5.2 %collective-permute-done.7 = bf16[128,1024]{1,0:T(8,128)(2,1)S(1)} collective-permute-done((bf16[128,1024]{1,0:T(8,128)(2,1)S(1)}, bf16[128,1024]{1,0:T(8,128)(2,1)S(1)}, u32[]{:S(2)}, u32[]{:S(2)}) %collective-permute-start.7) | collective-permute-done | bytes 262176 | tf_op jit(solution)/shard_map/ppermute | solution.py:21
  62.5 1.3 collective-permute-start.12
  63.8 0.2 fusion.46
  64.0 1.9 collective-permute-start.13
  66.0 1.7 constant_dynamic-update-slice_fusion.17
  67.7 0.0 collective-permute-done.9
  67.7 1.9 collective-permute-start.14
  69.6 1.7 constant_dynamic-update-slice_fusion.16
  71.3 1.9 collective-permute-start.15
  73.2 0.7 constant_dynamic-update-slice_fusion.15
  74.0 0.0 collective-permute-done.11
  74.0 0.8 constant_dynamic-update-slice_fusion.14
  74.7 22.1 %collective-permute-done.12 = bf16[128,1024]{0,1:T(8,128)(2,1)S(1)} collective-permute-done((bf16[128,1024]{0,1:T(8,128)(2,1)S(1)}, bf16[128,1024]{0,1:T(8,128)(2,1)S(1)}, u32[]{:S(2)}, u32[]{:S(2)}) %collective-permute-start.12) | collective-permute-done | bytes 262176 | tf_op jit(solution)/shard_map/ppermute | solution.py:21
  96.8 0.8 constant_dynamic-update-slice_fusion.13
  97.6 1.4 copy.11
  99.0 0.7 copy.17
  99.7 0.7 constant_dynamic-update-slice_fusion.12
  100.4 0.0 collective-permute-done.14
  100.4 1.7 constant_dynamic-update-slice_fusion.11
  102.2 1.7 constant_dynamic-update-slice_fusion.10
  103.9 0.7 constant_dynamic-update-slice_fusion.9
  104.6 1.9 fusion.47
  106.5 0.0 copy-start.4
  106.5 1.0 fusion.2
  107.5 1.8 fusion.4
  109.3 0.8 fusion.6
  110.1 0.4 copy-done.1
  110.5 1.1 fusion.35
  111.7 1.1 fusion.29
  112.8 4.8 %all-gather.3.cloned.1.call-done = bf16[1,2048,2688]{2,1,0:T(8,128)(2,1)} async-done(((bf16[1,256,2688]{2,1,0:T(8,128)(2,1)}), bf16[1,2048,2688]{2,1,0:T(8,128)(2,1)}) %all-gather.3.cloned.1.call-update) | async-done | bytes 11010064 | tf_op jit(solution)/shard_map/all_gather | solution.py:83
  117.6 6.0 %multiply_reduce_fusion = (f32[128]{0:T(128)S(1)}, f32[128,2688]{1,0:T(8,128)S(1)}) fusion(bf16[1,2048,2688]{2,1,0:T(8,128)(2,1)} %all-gather.3.cloned.1.call-done, bf16[128,1024]{0,1:T(8,128)(2,1)S(1)} %bitcast.111, bf16[128,1024]{0,1:T(8,128)(2,1)S(1)} %bitcast.110), kind=kOutput, calls=%fused_computation.27 | convolution fusion | flops 1411022720 | bytes 12911104 | tf_op jit(solution)/shard_map/dot_general | solution.py:81
  123.6 0.3 fusion.18
  123.9 3.4 %collective-permute-start.16 = (bf16[128,2688]{1,0:T(8,128)(2,1)S(1)}, bf16[128,2688]{1,0:T(8,128)(2,1)S(1)}, u32[]{:S(2)}, u32[]{:S(2)}) collective-permute-start(bf16[128,2688]{1,0:T(8,128)(2,1)S(1)} %fusion.18), channel_id=1, source_target_pairs={{0,8},{8,16},{16,24},{1,9},{9,17},{17,25},{2,10},{10,18},{18,26},{... | collective-permute-start | bytes 2064392 | tf_op jit(solution)/shard_map/ppermute | solution.py:21
  127.3 16.1 %collective-permute-done.16 = bf16[128,2688]{1,0:T(8,128)(2,1)S(1)} collective-permute-done((bf16[128,2688]{1,0:T(8,128)(2,1)S(1)}, bf16[128,2688]{1,0:T(8,128)(2,1)S(1)}, u32[]{:S(2)}, u32[]{:S(2)}) %collective-permute-start.16) | collective-permute-done | bytes 688160 | tf_op jit(solution)/shard_map/ppermute | solution.py:21
  143.4 1.3 fusion.25
  144.7 3.4 %collective-permute-start.17 = (bf16[128,2688]{1,0:T(8,128)(2,1)}, bf16[128,2688]{1,0:T(8,128)(2,1)S(1)}, u32[]{:S(2)}, u32[]{:S(2)}) collective-permute-start(bf16[128,2688]{1,0:T(8,128)(2,1)} %fusion.25), channel_id=1, source_target_pairs={{0,8},{8,16},{16,24},{1,9},{9,17},{17,25},{2,10},{10,18},{18,26},{... | collective-permute-start | bytes 2064392 | tf_op jit(solution)/shard_map/ppermute | solution.py:21
  148.1 15.4 %collective-permute-done.17 = bf16[128,2688]{1,0:T(8,128)(2,1)S(1)} collective-permute-done((bf16[128,2688]{1,0:T(8,128)(2,1)}, bf16[128,2688]{1,0:T(8,128)(2,1)S(1)}, u32[]{:S(2)}, u32[]{:S(2)}) %collective-permute-start.17) | collective-permute-done | bytes 688160 | tf_op jit(solution)/shard_map/ppermute | solution.py:21
  163.5 1.4 fusion.42
  165.0 3.4 %collective-permute-start.18 = (bf16[128,2688]{1,0:T(8,128)(2,1)}, bf16[128,2688]{1,0:T(8,128)(2,1)}, u32[]{:S(2)}, u32[]{:S(2)}) collective-permute-start(bf16[128,2688]{1,0:T(8,128)(2,1)} %fusion.42), channel_id=1, source_target_pairs={{0,8},{8,16},{16,24},{1,9},{9,17},{17,25},{2,10},{10,18},{18,26},{... | collective-permute-start | bytes 2064392 | tf_op jit(solution)/shard_map/ppermute | solution.py:21
  168.4 14.7 %collective-permute-done.18 = bf16[128,2688]{1,0:T(8,128)(2,1)} collective-permute-done((bf16[128,2688]{1,0:T(8,128)(2,1)}, bf16[128,2688]{1,0:T(8,128)(2,1)}, u32[]{:S(2)}, u32[]{:S(2)}) %collective-permute-start.18) | collective-permute-done | bytes 688160 | tf_op jit(solution)/shard_map/ppermute | solution.py:21
  183.0 2.7 %fusion.38 = bf16[1,128,2688]{2,1,0:T(8,128)(2,1)} fusion(f32[128,2688]{1,0:T(8,128)S(1)} %get-tuple-element.17, bf16[128,2688]{1,0:T(8,128)(2,1)} %collective-permute-done.18, f32[2688]{0:T(1024)S(1)} %convert_reduce_fusion, f32[128]{0:T(128)S(1)} %add_rsqrt_fusion, pred[]{:T(512)S(6)} %eq.12, bf16[128,2688]{1,0:T(8,128)(2,1)S(1)} %copy-done, pred[]{:T(512)S(6)} %eq.15, ...), kind=kLoop, calls=%fused_computation.36 | loop fusion | flops 5160960 | bytes 4828164 | tf_op jit(solution)/shard_map/broadcast_in_dim | solution.py:96
  (31 shorter events, 0.3 us)
Async XLA Ops:
  6.5 8.7 %copy-start.3 = (bf16[1,128,1024]{2,1,0:T(8,128)(2,1)S(1)}, bf16[1,128,1024]{2,1,0:T(8,128)(2,1)}, u32[]{:S(2)}) copy-start(bf16[1,128,1024]{2,1,0:T(8,128)(2,1)} %param.9) | copy-start | bytes 786436
  6.5 7.5 %copy-start.2 = (bf16[1,128,2048]{2,1,0:T(8,128)(2,1)S(1)}, bf16[1,128,2048]{2,1,0:T(8,128)(2,1)}, u32[]{:S(2)}) copy-start(bf16[1,128,2048]{2,1,0:T(8,128)(2,1)} %param.7) | copy-start | bytes 1572868
  6.5 7.6 %copy-start.5 = (bf16[1,2688]{1,0:T(2,128)(2,1)S(1)}, bf16[1,2688]{1,0:T(2,128)(2,1)}, u32[]{:S(2)}) copy-start(bf16[1,2688]{1,0:T(2,128)(2,1)} %param.11) | copy-start | bytes 16132
  6.5 111.1 %all-gather.3.cloned.1.call-start = ((), (), s32[]{:S(2)}) async-start(), calls=%async_computation | async-start | bytes 12386304 | tf_op jit(solution)/shard_map/all_gather | solution.py:83
  8.4 55.6 %collective-permute-start.8 = (bf16[128,1024]{0,1:T(8,128)(2,1)S(1)}, bf16[128,1024]{0,1:T(8,128)(2,1)}, u32[]{:S(2)}, u32[]{:S(2)}) collective-permute-start(bf16[128,1024]{0,1:T(8,128)(2,1)S(1)} %bitcast.101), channel_id=1, source_target_pairs={} | collective-permute-start | bytes 786440 | tf_op jit(solution)/shard_map/ppermute | solution.py:21
  9.7 57.9 %collective-permute-start.9 = (bf16[128,1024]{0,1:T(8,128)(2,1)S(1)}, bf16[128,1024]{0,1:T(8,128)(2,1)}, u32[]{:S(2)}, u32[]{:S(2)}) collective-permute-start(bf16[128,1024]{0,1:T(8,128)(2,1)S(1)} %bitcast.102), channel_id=1, source_target_pairs={{0,7},{8,15},{16,23},{24,31}} | collective-permute-start | bytes 786440 | tf_op jit(solution)/shard_map/ppermute | solution.py:21
  11.1 4.1 %collective-permute-start = (bf16[128,1024]{1,0:T(8,128)(2,1)}, bf16[128,1024]{1,0:T(8,128)(2,1)S(1)}, u32[]{:S(2)}, u32[]{:S(2)}) collective-permute-start(bf16[128,1024]{1,0:T(8,128)(2,1)} %bitcast.112), channel_id=1, source_target_pairs={} | collective-permute-start | bytes 786440 | tf_op jit(solution)/shard_map/ppermute | solution.py:21
  11.8 4.1 %collective-permute-start.1 = (bf16[128,1024]{1,0:T(8,128)(2,1)}, bf16[128,1024]{1,0:T(8,128)(2,1)S(1)}, u32[]{:S(2)}, u32[]{:S(2)}) collective-permute-start(bf16[128,1024]{1,0:T(8,128)(2,1)} %bitcast.113), channel_id=1, source_target_pairs={{0,7},{8,15},{16,23},{24,31}} | collective-permute-start | bytes 786440 | tf_op jit(solution)/shard_map/ppermute | solution.py:21
  12.4 4.8 %collective-permute-start.2 = (bf16[128,1024]{1,0:T(8,128)(2,1)}, bf16[128,1024]{1,0:T(8,128)(2,1)S(1)}, u32[]{:S(2)}, u32[]{:S(2)}) collective-permute-start(bf16[128,1024]{1,0:T(8,128)(2,1)} %bitcast.114), channel_id=1, source_target_pairs={{0,6},{1,7},{8,14},{9,15},{16,22},{17,23},{24,30},{25,31}} | collective-permute-start | bytes 786440 | tf_op jit(solution)/shard_map/ppermute | solution.py:21
  15.2 16.7 %collective-permute-start.3 = (bf16[128,1024]{1,0:T(8,128)(2,1)S(1)}, bf16[128,1024]{1,0:T(8,128)(2,1)S(1)}, u32[]{:S(2)}, u32[]{:S(2)}) collective-permute-start(bf16[128,1024]{1,0:T(8,128)(2,1)S(1)} %bitcast.115), channel_id=1, source_target_pairs={{0,5},{1,6},{2,7},{8,13},{9,14},{10,15},{16,21},{17,22},{18,23},{2... | collective-permute-start | bytes 786440 | tf_op jit(solution)/shard_map/ppermute | solution.py:21
  15.9 38.0 %collective-permute-start.4 = (bf16[128,1024]{1,0:T(8,128)(2,1)S(1)}, bf16[128,1024]{1,0:T(8,128)(2,1)S(1)}, u32[]{:S(2)}, u32[]{:S(2)}) collective-permute-start(bf16[128,1024]{1,0:T(8,128)(2,1)S(1)} %bitcast.116), channel_id=1, source_target_pairs={{0,4},{1,5},{2,6},{3,7},{8,12},{9,13},{10,14},{11,15},{16,20},{17,... | collective-permute-start | bytes 786440 | tf_op jit(solution)/shard_map/ppermute | solution.py:21
  17.3 38.6 %collective-permute-start.5 = (bf16[128,1024]{1,0:T(8,128)(2,1)S(1)}, bf16[128,1024]{1,0:T(8,128)(2,1)S(1)}, u32[]{:S(2)}, u32[]{:S(2)}) collective-permute-start(bf16[128,1024]{1,0:T(8,128)(2,1)S(1)} %bitcast.117), channel_id=1, source_target_pairs={{0,3},{1,4},{2,5},{3,6},{4,7},{8,11},{9,12},{10,13},{11,14},{12,15... | collective-permute-start | bytes 786440 | tf_op jit(solution)/shard_map/ppermute | solution.py:21
  31.9 24.7 %collective-permute-start.6 = (bf16[128,1024]{1,0:T(8,128)(2,1)S(1)}, bf16[128,1024]{1,0:T(8,128)(2,1)S(1)}, u32[]{:S(2)}, u32[]{:S(2)}) collective-permute-start(bf16[128,1024]{1,0:T(8,128)(2,1)S(1)} %bitcast.118), channel_id=1, source_target_pairs={{0,2},{1,3},{2,4},{3,5},{4,6},{5,7},{8,10},{9,11},{10,12},{11,13},... | collective-permute-start | bytes 786440 | tf_op jit(solution)/shard_map/ppermute | solution.py:21
  53.9 8.6 %collective-permute-start.7 = (bf16[128,1024]{1,0:T(8,128)(2,1)S(1)}, bf16[128,1024]{1,0:T(8,128)(2,1)S(1)}, u32[]{:S(2)}, u32[]{:S(2)}) collective-permute-start(bf16[128,1024]{1,0:T(8,128)(2,1)S(1)} %bitcast.119), channel_id=1, source_target_pairs={{0,1},{1,2},{2,3},{3,4},{4,5},{5,6},{6,7},{8,9},{9,10},{10,11},{11... | collective-permute-start | bytes 786440 | tf_op jit(solution)/shard_map/ppermute | solution.py:21
  55.9 15.4 %collective-permute-start.10 = (bf16[128,1024]{0,1:T(8,128)(2,1)S(1)}, bf16[128,1024]{0,1:T(8,128)(2,1)S(1)}, u32[]{:S(2)}, u32[]{:S(2)}) collective-permute-start(bf16[128,1024]{0,1:T(8,128)(2,1)S(1)} %bitcast.103), channel_id=1, source_target_pairs={{0,6},{1,7},{8,14},{9,15},{16,22},{17,23},{24,30},{25,31}} | collective-permute-start | bytes 786440 | tf_op jit(solution)/shard_map/ppermute | solution.py:21
  56.6 17.4 %collective-permute-start.11 = (bf16[128,1024]{0,1:T(8,128)(2,1)S(1)}, bf16[128,1024]{0,1:T(8,128)(2,1)S(1)}, u32[]{:S(2)}, u32[]{:S(2)}) collective-permute-start(bf16[128,1024]{0,1:T(8,128)(2,1)S(1)} %bitcast.104), channel_id=1, source_target_pairs={{0,5},{1,6},{2,7},{8,13},{9,14},{10,15},{16,21},{17,22},{18,23},{2... | collective-permute-start | bytes 786440 | tf_op jit(solution)/shard_map/ppermute | solution.py:21
  62.5 34.3 %collective-permute-start.12 = (bf16[128,1024]{0,1:T(8,128)(2,1)S(1)}, bf16[128,1024]{0,1:T(8,128)(2,1)S(1)}, u32[]{:S(2)}, u32[]{:S(2)}) collective-permute-start(bf16[128,1024]{0,1:T(8,128)(2,1)S(1)} %bitcast.105), channel_id=1, source_target_pairs={{0,4},{1,5},{2,6},{3,7},{8,12},{9,13},{10,14},{11,15},{16,20},{17,... | collective-permute-start | bytes 786440 | tf_op jit(solution)/shard_map/ppermute | solution.py:21
  64.0 35.7 %collective-permute-start.13 = (bf16[128,1024]{0,1:T(8,128)(2,1)S(1)}, bf16[128,1024]{0,1:T(8,128)(2,1)S(1)}, u32[]{:S(2)}, u32[]{:S(2)}) collective-permute-start(bf16[128,1024]{0,1:T(8,128)(2,1)S(1)} %bitcast.106), channel_id=1, source_target_pairs={{0,3},{1,4},{2,5},{3,6},{4,7},{8,11},{9,12},{10,13},{11,14},{12,15... | collective-permute-start | bytes 786440 | tf_op jit(solution)/shard_map/ppermute | solution.py:21
  67.7 32.8 %collective-permute-start.14 = (bf16[128,1024]{0,1:T(8,128)(2,1)S(1)}, bf16[128,1024]{0,1:T(8,128)(2,1)}, u32[]{:S(2)}, u32[]{:S(2)}) collective-permute-start(bf16[128,1024]{0,1:T(8,128)(2,1)S(1)} %bitcast.107), channel_id=1, source_target_pairs={{0,2},{1,3},{2,4},{3,5},{4,6},{5,7},{8,10},{9,11},{10,12},{11,13},... | collective-permute-start | bytes 786440 | tf_op jit(solution)/shard_map/ppermute | solution.py:21
  71.3 30.9 %collective-permute-start.15 = (bf16[128,1024]{0,1:T(8,128)(2,1)S(1)}, bf16[128,1024]{0,1:T(8,128)(2,1)}, u32[]{:S(2)}, u32[]{:S(2)}) collective-permute-start(bf16[128,1024]{0,1:T(8,128)(2,1)S(1)} %bitcast.108), channel_id=1, source_target_pairs={{0,1},{1,2},{2,3},{3,4},{4,5},{5,6},{6,7},{8,9},{9,10},{10,11},{11... | collective-permute-start | bytes 786440 | tf_op jit(solution)/shard_map/ppermute | solution.py:21
  106.5 1.0 copy-start.4
  109.3 1.3 copy-start.1
  117.6 6.0 %copy-start = (bf16[128,2688]{1,0:T(8,128)(2,1)S(1)}, bf16[128,2688]{1,0:T(8,128)(2,1)}, u32[]{:S(2)}) copy-start(bf16[128,2688]{1,0:T(8,128)(2,1)} %param.6) | copy-start | bytes 2064388
  123.9 19.5 %collective-permute-start.16 = (bf16[128,2688]{1,0:T(8,128)(2,1)S(1)}, bf16[128,2688]{1,0:T(8,128)(2,1)S(1)}, u32[]{:S(2)}, u32[]{:S(2)}) collective-permute-start(bf16[128,2688]{1,0:T(8,128)(2,1)S(1)} %fusion.18), channel_id=1, source_target_pairs={{0,8},{8,16},{16,24},{1,9},{9,17},{17,25},{2,10},{10,18},{18,26},{... | collective-permute-start | bytes 2064392 | tf_op jit(solution)/shard_map/ppermute | solution.py:21
  144.7 18.8 %collective-permute-start.17 = (bf16[128,2688]{1,0:T(8,128)(2,1)}, bf16[128,2688]{1,0:T(8,128)(2,1)S(1)}, u32[]{:S(2)}, u32[]{:S(2)}) collective-permute-start(bf16[128,2688]{1,0:T(8,128)(2,1)} %fusion.25), channel_id=1, source_target_pairs={{0,8},{8,16},{16,24},{1,9},{9,17},{17,25},{2,10},{10,18},{18,26},{... | collective-permute-start | bytes 2064392 | tf_op jit(solution)/shard_map/ppermute | solution.py:21
  165.0 18.1 %collective-permute-start.18 = (bf16[128,2688]{1,0:T(8,128)(2,1)}, bf16[128,2688]{1,0:T(8,128)(2,1)}, u32[]{:S(2)}, u32[]{:S(2)}) collective-permute-start(bf16[128,2688]{1,0:T(8,128)(2,1)} %fusion.42), channel_id=1, source_target_pairs={{0,8},{8,16},{16,24},{1,9},{9,17},{17,25},{2,10},{10,18},{18,26},{... | collective-permute-start | bytes 2064392 | tf_op jit(solution)/shard_map/ppermute | solution.py:21
Sparse Core Ops, SparseCore 0:
  9.2 108.3 all-gather.2
where the time goes:
time: 193 us
  waiting for transfers between devices  89.3 us (46%)
  starting transfers between devices  53.4 us (28%)
  local copies, waits for them, and re-layouts  17.5 us (9%)
  between operations  13.8 us (7%)
  matrix products  11 us (6%)
  other arithmetic  7.49 us (4%)
    ppermute x19, waiting for transfers between devices, passed_along(): return lax.ppermute(block, axis, route)  83.8 us
    ppermute x19, starting transfers between devices, passed_along(): return lax.ppermute(block, axis, route)  53.4 us
    unnamed x31, local copies, waits for them, and re-layouts  12.6 us
    dot_general x1, matrix products, local(): jnp.dot(attended, lax.all_gather(out_weight[0], 'ctx', axis=0, tiled=True...  5.97 us
    all_gather x1, waiting for transfers between devices, local(): lax.all_gather(out_weight[0], 'ctx', axis=0, tiled=True)  4.78 us
  transfers between devices with their start and end apart: 20, of which 7 were waited for; matrix products, arithmetic and copies ran while one was open for 12% of the time, Pallas kernels for 0%

commit v1 on v0

--- a/solution.py
+++ b/solution.py
@@ -1,8 +1,11 @@
+import functools
 import math
 
 import jax
 import jax.numpy as jnp
 from jax import lax
+from jax.experimental import pallas as pl
+from jax.experimental.pallas import tpu as pltpu
 from jax.sharding import PartitionSpec as P
 
 KEY_HEADS = 8
@@ -96,6 +99,375 @@
     return running.astype(jnp.bfloat16)[None]
 
 
+LANES = 128
+MESH = pl.DeviceIdType.MESH
+CHUNKS = 4
+
+
+def column_tiles(start, stop, width):
+    return [(at, min(at + width, stop) - at) for at in range(start, stop, width)]
+
+
+def fused_kernel(
+    sections,
+    chunks,
+    half,
+    gains_ref,
+    stream_ref,
+    q_ref,
+    k_ref,
+    v_ref,
+    w_hbm,
+    out_ref,
+    qbuf,
+    kbuf,
+    vbuf,
+    w_ref,
+    att,
+    pair_out,
+    pair_in,
+    x1_out,
+    x1_in,
+    y1_out,
+    y1_in,
+    x2_out,
+    x2_in,
+    y2_out,
+    y2_in,
+    keep_me,
+    keep_x,
+    keep_y,
+    base,
+    local_sem,
+    a2a_send,
+    a2a_recv,
+    pair_sem,
+    x1_sem,
+    y1_sem,
+    x2_sem,
+    y2_sem,
+    chain_sem,
+):
+    me = lax.axis_index("ctx")
+    section = lax.axis_index("section")
+    devices, rows, query_width = qbuf.shape
+    width = w_ref.shape[1]
+    chunk_rows = rows // chunks
+    quarter, pair_count = devices // 4, devices // 2
+    core = me % 2
+    across = (me // quarter) % 2
+    up = me // pair_count
+    flips = (1 - 2 * core, quarter * (1 - 2 * across), pair_count * (1 - 2 * up))
+
+    def peer(flip_core, flip_x, flip_y):
+        return me + flips[0] * flip_core + flips[1] * flip_x + flips[2] * flip_y
+
+    sibling, beside, above, diagonal = peer(1, 0, 0), peer(0, 1, 0), peer(0, 0, 1), peer(0, 1, 1)
+    has_prev = jnp.minimum(section, 1)
+    has_next = jnp.minimum(sections - 1 - section, 1)
+
+    def own_rows(buf):
+        return buf.at[pl.ds(pl.multiple_of(me * rows, rows), rows)]
+
+    def head_columns(ref, who, span):
+        return ref.at[:, pl.ds(pl.multiple_of(who * span, span), span)]
+
+    w_copy = pltpu.make_async_copy(w_hbm, w_ref, local_sem.at[0])
+    w_copy.start()
+
+    @pl.when(section == 0)
+    def _():
+        for chunk in range(chunks):
+            pltpu.make_async_copy(
+                stream_ref.at[pl.ds(chunk * chunk_rows, chunk_rows)],
+                base.at[chunk],
+                chain_sem.at[1, chunk],
+            ).start()
+
+    own = [
+        (head_columns(q_ref, me, query_width), qbuf.at[me], 0),
+        (head_columns(k_ref, me, HEAD_WIDTH), own_rows(kbuf), 1),
+        (head_columns(v_ref, me, HEAD_WIDTH), own_rows(vbuf), 2),
+    ]
+    for source, target, which in own:
+        pltpu.make_async_copy(source, target, a2a_recv.at[which, me]).start()
+
+    order = [(0, 1, 1), (1, 1, 1), (0, 1, 0), (0, 0, 1), (1, 1, 0), (1, 0, 1), (1, 0, 0)]
+    barrier = pltpu.get_barrier_semaphore()
+    for flip in order:
+        pl.semaphore_signal(barrier, inc=1, device_id=(section, peer(*flip)), device_id_type=MESH)
+
+    @pl.when(section > 0)
+    def _():
+        pl.semaphore_signal(barrier, inc=1, device_id=(section - 1, me), device_id_type=MESH)
+
+    @pl.when(section < sections - 1)
+    def _():
+        pl.semaphore_signal(barrier, inc=1, device_id=(section + 1, me), device_id_type=MESH)
+
+    pl.semaphore_wait(barrier, len(order) + has_prev + has_next)
+
+    def exchange(who):
+        return [
+            pltpu.make_async_remote_copy(
+                src_ref=source,
+                dst_ref=target,
+                send_sem=a2a_send.at[which, who],
+                recv_sem=a2a_recv.at[which, me],
+                device_id=(section, who),
+                device_id_type=MESH,
+            )
+            for source, target, which in (
+                (head_columns(k_ref, who, HEAD_WIDTH), own_rows(kbuf), 1),
+                (head_columns(v_ref, who, HEAD_WIDTH), own_rows(vbuf), 2),
+                (head_columns(q_ref, who, query_width), qbuf.at[me], 0),
+            )
+        ]
+
+    for flip in order:
+        for copy in exchange(peer(*flip)):
+            copy.start()
+
+    def arrive(block):
+        for which, target in (
+            (0, qbuf.at[block]),
+            (1, kbuf.at[pl.ds(block * rows, rows)]),
+            (2, vbuf.at[pl.ds(block * rows, rows)]),
+        ):
+            pltpu.make_async_copy(target, target, a2a_recv.at[which, block]).wait()
+
+    factor = QUERY_SCALAR ** (-0.5) * math.log2(math.e)
+    seen = lax.broadcasted_iota(jnp.int32, (rows, rows), 1) <= lax.broadcasted_iota(
+        jnp.int32, (rows, rows), 0
+    )
+    for block in range(devices):
+        arrive(block)
+        reach = (block + 1) * rows
+        for head in range(query_width // HEAD_WIDTH):
+            columns = slice(head * HEAD_WIDTH, (head + 1) * HEAD_WIDTH)
+            scores = lax.dot_general(
+                qbuf[block, :, columns],
+                kbuf[0:reach],
+                (((1,), (1,)), ((), ())),
+                preferred_element_type=jnp.float32,
+            )
+            last = jnp.where(seen, scores[:, block * rows :], -jnp.inf)
+            if block:
+                scores = jnp.concatenate([scores[:, : block * rows], last], axis=1)
+            else:
+                scores = last
+            top = jnp.max(scores, axis=1, keepdims=True)
+            exponent = jnp.exp2((scores - top) * factor)
+            total = jnp.sum(exponent, axis=1, keepdims=True)
+            mixed = jnp.dot(
+                exponent.astype(jnp.bfloat16), vbuf[0:reach], preferred_element_type=jnp.float32
+            )
+            mixed = (mixed / total).astype(jnp.bfloat16)
+            for chunk in range(chunks):
+                att[block % 2, chunk, block // 2, :, columns] = mixed[
+                    chunk * chunk_rows : (chunk + 1) * chunk_rows
+                ]
+
+    w_copy.wait()
+
+    def remote(source, target, sems, chunk, who):
+        return pltpu.make_async_remote_copy(
+            src_ref=source.at[chunk],
+            dst_ref=target.at[chunk],
+            send_sem=sems.at[0, chunk],
+            recv_sem=sems.at[1, chunk],
+            device_id=who,
+            device_id_type=MESH,
+        )
+
+    def pair_copy(chunk):
+        return remote(pair_out, pair_in, pair_sem, chunk, (section, sibling))
+
+    def x1_copy(chunk):
+        return remote(x1_out, x1_in, x1_sem, chunk, (section, beside))
+
+    def y1_copy(chunk):
+        return remote(y1_out, y1_in, y1_sem, chunk, (section, above))
+
+    def x2_copy(chunk):
+        return remote(x2_out, x2_in, x2_sem, chunk, (section, beside))
+
+    def y2_copy(chunk):
+        return remote(y2_out, y2_in, y2_sem, chunk, (section, above))
+
+    def chain_copy(chunk):
+        return pltpu.make_async_remote_copy(
+            src_ref=out_ref.at[chunk],
+            dst_ref=base.at[chunk],
+            send_sem=chain_sem.at[0, chunk],
+            recv_sem=chain_sem.at[1, chunk],
+            device_id=(jnp.minimum(section + 1, sections - 1), me),
+            device_id_type=MESH,
+        )
+
+    chip_count = pair_count
+    places = [who // 2 for who in (beside, diagonal, above, me)]
+
+    def for_sibling(chunk):
+        left = att[1 - core, chunk].reshape(chip_count * chunk_rows, query_width)
+        for at, span in column_tiles(0, width, 512):
+            part = jnp.dot(left, w_ref[:, at : at + span], preferred_element_type=jnp.float32)
+            pair_out[chunk, :, :, at : at + span] = part.astype(jnp.bfloat16).reshape(
+                chip_count, chunk_rows, span
+            )
+        pair_copy(chunk).start()
+
+    def first_turn(chunk):
+        pair_copy(chunk).wait_recv()
+        left = jnp.concatenate([att[core, chunk, place] for place in places], axis=0)
+
+        def summed(at, span):
+            part = jnp.dot(left, w_ref[:, at : at + span], preferred_element_type=jnp.float32)
+            return [
+                part[index * chunk_rows : (index + 1) * chunk_rows]
+                + pair_in[chunk, place, :, at : at + span].astype(jnp.float32)
+                for index, place in enumerate(places)
+            ]
+
+        for at, span in column_tiles(0, half, 512):
+            to_beside, to_diagonal, to_above, mine = summed(at, span)
+            x1_out[chunk, 0, :, at : at + span] = to_beside.astype(jnp.bfloat16)
+            x1_out[chunk, 1, :, at : at + span] = to_diagonal.astype(jnp.bfloat16)
+            keep_y[chunk, :, at : at + span] = to_above
+            keep_me[chunk, :, at : at + span] = mine
+        x1_copy(chunk).start()
+        for at, span in column_tiles(half, width, 512):
+            to_beside, to_diagonal, to_above, mine = summed(at, span)
+            y1_out[chunk, 0, :, at - half : at - half + span] = to_above.astype(jnp.bfloat16)
+            y1_out[chunk, 1, :, at - half : at - half + span] = to_diagonal.astype(jnp.bfloat16)
+            keep_x[chunk, :, at - half : at - half + span] = to_beside
+            keep_me[chunk, :, at : at + span] = mine
+        y1_copy(chunk).start()
+
+    def second_turn(chunk):
+        x1_copy(chunk).wait_recv()
+        y2_out[chunk] = (keep_y[chunk] + x1_in[chunk, 1].astype(jnp.float32)).astype(jnp.bfloat16)
+        y2_copy(chunk).start()
+        y1_copy(chunk).wait_recv()
+        x2_out[chunk] = (keep_x[chunk] + y1_in[chunk, 1].astype(jnp.float32)).astype(jnp.bfloat16)
+        x2_copy(chunk).start()
+        keep_me[chunk, :, :half] += x1_in[chunk, 0].astype(jnp.float32)
+        keep_me[chunk, :, half:] += y1_in[chunk, 0].astype(jnp.float32)
+
+    def normalise(chunk):
+        y2_copy(chunk).wait_recv()
+        x2_copy(chunk).wait_recv()
+        low = keep_me[chunk, :, :half] + y2_in[chunk].astype(jnp.float32)
+        high = keep_me[chunk, :, half:] + x2_in[chunk].astype(jnp.float32)
+        squares = jnp.sum(low * low, axis=1, keepdims=True) + jnp.sum(
+            high * high, axis=1, keepdims=True
+        )
+        ratio = lax.rsqrt(squares * (1.0 / width) + norm_eps)
+        keep_me[chunk, :, :half] = low * ratio * gains_ref[:, :half].astype(jnp.float32)
+        keep_me[chunk, :, half:] = high * ratio * gains_ref[:, half:].astype(jnp.float32)
+
+    def hand_on(chunk):
+        pltpu.make_async_copy(base.at[chunk], base.at[chunk], chain_sem.at[1, chunk]).wait()
+        out_ref[chunk] = (base[chunk].astype(jnp.float32) + keep_me[chunk]).astype(out_ref.dtype)
+
+        @pl.when(section < sections - 1)
+        def _():
+            chain_copy(chunk).start()
+
+    def turn(step, carry):
+        for lag, stage in enumerate((for_sibling, first_turn, second_turn, normalise)):
+            chunk = step - lag
+
+            @pl.when((chunk >= 0) & (chunk < chunks))
+            def _():
+                stage(chunk)
+
+        passed = step - 3 - section
+
+        @pl.when((passed >= 0) & (passed < chunks))
+        def _():
+            hand_on(passed)
+
+        return carry
+
+    lax.fori_loop(0, chunks + 3 + sections - 1, turn, 0)
+
+    for flip in order:
+        for copy in exchange(peer(*flip)):
+            copy.wait_send()
+
+    def finish(chunk, carry):
+        for copy in (pair_copy, x1_copy, y1_copy, x2_copy, y2_copy):
+            copy(chunk).wait_send()
+
+        @pl.when(section < sections - 1)
+        def _():
+            chain_copy(chunk).wait_send()
+
+        return carry
+
+    lax.fori_loop(0, chunks, finish, 0)
+
+
+def by_head(sections, chunks, stream, queries, keys, values, out_weight, gains):
+    devices = lax.axis_size("ctx")
+    rows, width = stream.shape
+    query_width = queries.shape[2] // devices
+    chunk_rows = rows // chunks
+    half = (width // LANES + 1) // 2 * LANES
+    other = width - half
+    chips = devices // 2
+    narrow, wide = jnp.bfloat16, jnp.float32
+    anywhere = pl.BlockSpec(memory_space=pl.ANY)
+    in_vmem = pl.BlockSpec(memory_space=pltpu.VMEM)
+    dma = pltpu.SemaphoreType.DMA
+    out = pl.pallas_call(
+        functools.partial(fused_kernel, sections, chunks, half),
+        out_shape=jax.ShapeDtypeStruct((chunks, chunk_rows, width), narrow),
+        in_specs=[in_vmem] + [anywhere] * 5,
+        out_specs=in_vmem,
+        scratch_shapes=[
+            pltpu.VMEM((devices, rows, query_width), narrow),
+            pltpu.VMEM((devices * rows, HEAD_WIDTH), narrow),
+            pltpu.VMEM((devices * rows, HEAD_WIDTH), narrow),
+            pltpu.VMEM(out_weight.shape[1:], narrow),
+            pltpu.VMEM((2, chunks, chips, chunk_rows, query_width), narrow),
+            pltpu.VMEM((chunks, chips, chunk_rows, width), narrow),
+            pltpu.VMEM((chunks, chips, chunk_rows, width), narrow),
+            pltpu.VMEM((chunks, 2, chunk_rows, half), narrow),
+            pltpu.VMEM((chunks, 2, chunk_rows, half), narrow),
+            pltpu.VMEM((chunks, 2, chunk_rows, other), narrow),
+            pltpu.VMEM((chunks, 2, chunk_rows, other), narrow),
+            pltpu.VMEM((chunks, chunk_rows, other), narrow),
+            pltpu.VMEM((chunks, chunk_rows, other), narrow),
+            pltpu.VMEM((chunks, chunk_rows, half), narrow),
+            pltpu.VMEM((chunks, chunk_rows, half), narrow),
+            pltpu.VMEM((chunks, chunk_rows, width), wide),
+            pltpu.VMEM((chunks, chunk_rows, other), wide),
+            pltpu.VMEM((chunks, chunk_rows, half), wide),
+            pltpu.VMEM((chunks, chunk_rows, width), narrow),
+            dma((1,)),
+            dma((3, devices)),
+            dma((3, devices)),
+            dma((2, chunks)),
+            dma((2, chunks)),
+            dma((2, chunks)),
+            dma((2, chunks)),
+            dma((2, chunks)),
+            dma((2, chunks)),
+        ],
+        compiler_params=pltpu.CompilerParams(
+            collective_id=0, has_side_effects=True, vmem_limit_bytes=48 * 1024 * 1024
+        ),
+    )(gains, stream, queries[0], keys[0], values[0], out_weight[0])
+    return out.reshape(1, rows, width)
+
+
+def fits_by_head(mesh, rows):
+    devices = mesh.shape["ctx"]
+    return devices == KEY_HEADS and devices * rows <= WINDOW_LENGTH and devices % 8 == 0
+
+
 def solution(mesh):
     in_specs = (
         P("ctx", None),
@@ -106,4 +478,12 @@
         P("section", None),
     )
     out_specs = P("section", "ctx", None)
-    return jax.shard_map(local, mesh=mesh, in_specs=in_specs, out_specs=out_specs, check_vma=False)
+    sections = mesh.shape["section"]
+
+    def step(stream, *rest):
+        rows = stream.shape[0]
+        if fits_by_head(mesh, rows):
+            return by_head(sections, CHUNKS, stream, *rest)
+        return local(stream, *rest)
+
+    return jax.shard_map(step, mesh=mesh, in_specs=in_specs, out_specs=out_specs, check_vma=False)

time: 193 us -> 71.6 us (0.37)
  the two profiles are of different devices: /device:TPU:12 before, /device:TPU:24 now
where the time goes in v1:
time: 71.6 us; the launch traced here: 71.3 us
  Pallas kernels  64.3 us (90%)
  local copies, waits for them, and re-layouts  6.93 us (10%)
    pallas_call x1, Pallas kernels, by_head(): pl.pallas_call(functools.partial(fused_kernel, sections, chunks, half), o...  64.3 us
    unnamed x13, local copies, waits for them, and re-layouts  6.93 us

profile of v1, /device:TPU:24, one launch (start us, length us, event | category | flops | bytes accessed | tf_op | source)
XLA Modules:
  0.0 71.3 jit_solution(8261862534067252782)
XLA Ops:
  0.0 0.0 copy-start
  0.0 1.3 %copy-done = bf16[1,256,2688]{2,1,0:T(8,128)(2,1)S(1)} copy-done((bf16[1,256,2688]{2,1,0:T(8,128)(2,1)S(1)}, bf16[1,256,2688]{2,1,0:T(8,128)(2,1)}, u32[]{:S(2)}) %copy-start) | copy-done | bytes 1376280
  1.3 0.0 copy-start.1
  1.3 1.1 %copy-done.1 = bf16[128,2688]{1,0:T(8,128)(2,1)S(1)} copy-done((bf16[128,2688]{1,0:T(8,128)(2,1)S(1)}, bf16[128,2688]{1,0:T(8,128)(2,1)}, u32[]{:S(2)}) %copy-start.1) | copy-done | bytes 688152
  2.4 0.0 copy-start.2
  2.4 1.0 %copy-done.2 = bf16[1,128,2048]{2,1,0:T(8,128)(2,1)S(1)} copy-done((bf16[1,128,2048]{2,1,0:T(8,128)(2,1)S(1)}, bf16[1,128,2048]{2,1,0:T(8,128)(2,1)}, u32[]{:S(2)}) %copy-start.2) | copy-done | bytes 524312
  3.5 0.0 copy-start.3
  3.5 0.9 %copy-done.3 = bf16[1,128,1024]{2,1,0:T(8,128)(2,1)S(1)} copy-done((bf16[1,128,1024]{2,1,0:T(8,128)(2,1)S(1)}, bf16[1,128,1024]{2,1,0:T(8,128)(2,1)}, u32[]{:S(2)}) %copy-start.3) | copy-done | bytes 262168
  4.4 0.0 copy-start.4
  4.4 0.9 %copy-done.4 = bf16[1,128,1024]{2,1,0:T(8,128)(2,1)S(1)} copy-done((bf16[1,128,1024]{2,1,0:T(8,128)(2,1)S(1)}, bf16[1,128,1024]{2,1,0:T(8,128)(2,1)}, u32[]{:S(2)}) %copy-start.4) | copy-done | bytes 262168
  5.4 0.0 copy-start.5
  5.4 0.7 copy-done.5
  6.1 64.3 %shard_map.64 = bf16[4,32,2688]{2,1,0:T(8,128)(2,1)S(1)} custom-call(bf16[1,2688]{1,0:T(2,128)(2,1)S(1)} %copy-done.5, bf16[128,2688]{1,0:T(8,128)(2,1)S(1)} %copy-done.1, bf16[128,2048]{1,0:T(8,128)(2,1)S(1)} %bitcast.7, bf16[128,1024]{1,0:T(8,128)(2,1)S(1)} %bitcast.8, bf16[128,1024]{1,0:T(8,128)(2,1)S(1)} %bitcast.9, bf16[256,2688]{1,0:T(8,128)(2,1)S(1)} %bitcast.6), custom_call_target="tpu_custom_call" | custom-call | tf_op jit(solution)/shard_map/pallas_call | solution.py:424
  70.4 0.8 %copy.8 = bf16[1,128,2688]{2,1,0:T(8,128)(2,1)} copy(bf16[1,128,2688]{2,1,0:T(8,128)(2,1)S(1)} %bitcast.5) | data formatting | bytes 1376256
Async XLA Ops:
  0.0 1.3 %copy-start = (bf16[1,256,2688]{2,1,0:T(8,128)(2,1)S(1)}, bf16[1,256,2688]{2,1,0:T(8,128)(2,1)}, u32[]{:S(2)}) copy-start(bf16[1,256,2688]{2,1,0:T(8,128)(2,1)} %param.10) | copy-start | bytes 4128772
  1.3 1.1 %copy-start.1 = (bf16[128,2688]{1,0:T(8,128)(2,1)S(1)}, bf16[128,2688]{1,0:T(8,128)(2,1)}, u32[]{:S(2)}) copy-start(bf16[128,2688]{1,0:T(8,128)(2,1)} %stream_ref.1) | copy-start | bytes 2064388
  2.4 1.0 %copy-start.2 = (bf16[1,128,2048]{2,1,0:T(8,128)(2,1)S(1)}, bf16[1,128,2048]{2,1,0:T(8,128)(2,1)}, u32[]{:S(2)}) copy-start(bf16[1,128,2048]{2,1,0:T(8,128)(2,1)} %param.7) | copy-start | bytes 1572868
  3.5 0.9 %copy-start.3 = (bf16[1,128,1024]{2,1,0:T(8,128)(2,1)S(1)}, bf16[1,128,1024]{2,1,0:T(8,128)(2,1)}, u32[]{:S(2)}) copy-start(bf16[1,128,1024]{2,1,0:T(8,128)(2,1)} %param.8) | copy-start | bytes 786436
  4.4 0.9 %copy-start.4 = (bf16[1,128,1024]{2,1,0:T(8,128)(2,1)S(1)}, bf16[1,128,1024]{2,1,0:T(8,128)(2,1)}, u32[]{:S(2)}) copy-start(bf16[1,128,1024]{2,1,0:T(8,128)(2,1)} %param.9) | copy-start | bytes 786436
  5.4 0.7 copy-start.5

commit v2 on v1

--- a/solution.py
+++ b/solution.py
@@ -101,7 +101,10 @@
 
 LANES = 128
 MESH = pl.DeviceIdType.MESH
-CHUNKS = 4
+CHUNKS = 8
+PARTS = 2
+LEAD = 2
+VMEM_GRANT = 66_300_000
 
 
 def column_tiles(start, stop, width):
@@ -111,8 +114,9 @@
 def fused_kernel(
     sections,
     chunks,
+    parts,
     half,
-    gains_ref,
+    gains_hbm,
     stream_ref,
     q_ref,
     k_ref,
@@ -123,6 +127,7 @@
     kbuf,
     vbuf,
     w_ref,
+    gains_ref,
     att,
     pair_out,
     pair_in,
@@ -174,6 +179,8 @@
 
     w_copy = pltpu.make_async_copy(w_hbm, w_ref, local_sem.at[0])
     w_copy.start()
+    gains_copy = pltpu.make_async_copy(gains_hbm, gains_ref, local_sem.at[1])
+    gains_copy.start()
 
     @pl.when(section == 0)
     def _():
@@ -184,12 +191,22 @@
                 chain_sem.at[1, chunk],
             ).start()
 
-    own = [
-        (head_columns(q_ref, me, query_width), qbuf.at[me], 0),
-        (head_columns(k_ref, me, HEAD_WIDTH), own_rows(kbuf), 1),
-        (head_columns(v_ref, me, HEAD_WIDTH), own_rows(vbuf), 2),
-    ]
-    for source, target, which in own:
+    part_rows = rows // parts
+
+    def query_part(who, part):
+        source = q_ref.at[
+            pl.ds(part * part_rows, part_rows),
+            pl.ds(pl.multiple_of(who * query_width, query_width), query_width),
+        ]
+        return source, qbuf.at[me, pl.ds(part * part_rows, part_rows)]
+
+    def pieces(who):
+        return [
+            (head_columns(k_ref, who, HEAD_WIDTH), own_rows(kbuf)),
+            (head_columns(v_ref, who, HEAD_WIDTH), own_rows(vbuf)),
+        ] + [query_part(who, part) for part in range(parts)]
+
+    for which, (source, target) in enumerate(pieces(me)):
         pltpu.make_async_copy(source, target, a2a_recv.at[which, me]).start()
 
     order = [(0, 1, 1), (1, 1, 1), (0, 1, 0), (0, 0, 1), (1, 1, 0), (1, 0, 1), (1, 0, 0)]
@@ -217,36 +234,44 @@
                 device_id=(section, who),
                 device_id_type=MESH,
             )
-            for source, target, which in (
-                (head_columns(k_ref, who, HEAD_WIDTH), own_rows(kbuf), 1),
-                (head_columns(v_ref, who, HEAD_WIDTH), own_rows(vbuf), 2),
-                (head_columns(q_ref, who, query_width), qbuf.at[me], 0),
+            for which, (source, target) in enumerate(pieces(who))
+        ]
+
+    exchanges = [exchange(peer(*flip)) for flip in order]
+    for wave in zip(*exchanges):
+        for copy in wave:
+            copy.start()
+
+    def arrive(which, target, block):
+        pltpu.make_async_copy(target, target, a2a_recv.at[which, block]).wait()
+
+    factor = QUERY_SCALAR ** (-0.5) * math.log2(math.e)
+    group = query_width // HEAD_WIDTH
+    part_chunks = chunks // parts
+
+    def attend(part):
+        low = pl.multiple_of(part * part_rows, part_rows)
+        place = lax.broadcasted_iota(jnp.int32, (group, part_rows, rows), 1) + low
+        seen = lax.broadcasted_iota(jnp.int32, (group, part_rows, rows), 2) <= place
+        seen = seen.reshape(group * part_rows, rows)
+        for block in range(devices):
+
+            @pl.when(part == 0)
+            def _():
+                arrive(0, kbuf.at[pl.ds(block * rows, rows)], block)
+                arrive(1, vbuf.at[pl.ds(block * rows, rows)], block)
+
+            arrive(2 + part, qbuf.at[block, pl.ds(low, part_rows)], block)
+            reach = (block + 1) * rows
+            asked = jnp.concatenate(
+                [
+                    qbuf[block, pl.ds(low, part_rows), head * HEAD_WIDTH : (head + 1) * HEAD_WIDTH]
+                    for head in range(group)
+                ],
+                axis=0,
             )
-        ]
-
-    for flip in order:
-        for copy in exchange(peer(*flip)):
-            copy.start()
-
-    def arrive(block):
-        for which, target in (
-            (0, qbuf.at[block]),
-            (1, kbuf.at[pl.ds(block * rows, rows)]),
-            (2, vbuf.at[pl.ds(block * rows, rows)]),
-        ):
-            pltpu.make_async_copy(target, target, a2a_recv.at[which, block]).wait()
-
-    factor = QUERY_SCALAR ** (-0.5) * math.log2(math.e)
-    seen = lax.broadcasted_iota(jnp.int32, (rows, rows), 1) <= lax.broadcasted_iota(
-        jnp.int32, (rows, rows), 0
-    )
-    for block in range(devices):
-        arrive(block)
-        reach = (block + 1) * rows
-        for head in range(query_width // HEAD_WIDTH):
-            columns = slice(head * HEAD_WIDTH, (head + 1) * HEAD_WIDTH)
             scores = lax.dot_general(
-                qbuf[block, :, columns],
+                asked,
                 kbuf[0:reach],
                 (((1,), (1,)), ((), ())),
                 preferred_element_type=jnp.float32,
@@ -263,12 +288,16 @@
                 exponent.astype(jnp.bfloat16), vbuf[0:reach], preferred_element_type=jnp.float32
             )
             mixed = (mixed / total).astype(jnp.bfloat16)
-            for chunk in range(chunks):
-                att[block % 2, chunk, block // 2, :, columns] = mixed[
-                    chunk * chunk_rows : (chunk + 1) * chunk_rows
-                ]
-
-    w_copy.wait()
+            for head in range(group):
+                for chunk in range(part_chunks):
+                    start = head * part_rows + chunk * chunk_rows
+                    att[
+                        block % 2,
+                        part * part_chunks + chunk,
+                        block // 2,
+                        :,
+                        head * HEAD_WIDTH : (head + 1) * HEAD_WIDTH,
+                    ] = mixed[start : start + chunk_rows]
 
     def remote(source, target, sems, chunk, who):
         return pltpu.make_async_remote_copy(
@@ -374,7 +403,18 @@
         def _():
             chain_copy(chunk).start()
 
-    def turn(step, carry):
+    def turn(ahead, carry):
+        step = ahead - LEAD
+
+        @pl.when((ahead % part_chunks == 0) & (ahead < chunks))
+        def _():
+            attend(ahead // part_chunks)
+
+        @pl.when(step == 0)
+        def _():
+            w_copy.wait()
+            gains_copy.wait()
+
         for lag, stage in enumerate((for_sibling, first_turn, second_turn, normalise)):
             chunk = step - lag
 
@@ -390,10 +430,10 @@
 
         return carry
 
-    lax.fori_loop(0, chunks + 3 + sections - 1, turn, 0)
-
-    for flip in order:
-        for copy in exchange(peer(*flip)):
+    lax.fori_loop(0, LEAD + chunks + 3 + sections - 1, turn, 0)
+
+    for wave in exchanges:
+        for copy in wave:
             copy.wait_send()
 
     def finish(chunk, carry):
@@ -409,7 +449,7 @@
     lax.fori_loop(0, chunks, finish, 0)
 
 
-def by_head(sections, chunks, stream, queries, keys, values, out_weight, gains):
+def by_head(sections, chunks, parts, stream, queries, keys, values, out_weight, gains):
     devices = lax.axis_size("ctx")
     rows, width = stream.shape
     query_width = queries.shape[2] // devices
@@ -422,15 +462,16 @@
     in_vmem = pl.BlockSpec(memory_space=pltpu.VMEM)
     dma = pltpu.SemaphoreType.DMA
     out = pl.pallas_call(
-        functools.partial(fused_kernel, sections, chunks, half),
+        functools.partial(fused_kernel, sections, chunks, parts, half),
         out_shape=jax.ShapeDtypeStruct((chunks, chunk_rows, width), narrow),
-        in_specs=[in_vmem] + [anywhere] * 5,
+        in_specs=[anywhere] * 6,
         out_specs=in_vmem,
         scratch_shapes=[
             pltpu.VMEM((devices, rows, query_width), narrow),
             pltpu.VMEM((devices * rows, HEAD_WIDTH), narrow),
             pltpu.VMEM((devices * rows, HEAD_WIDTH), narrow),
             pltpu.VMEM(out_weight.shape[1:], narrow),
+            pltpu.VMEM(gains.shape, narrow),
             pltpu.VMEM((2, chunks, chips, chunk_rows, query_width), narrow),
             pltpu.VMEM((chunks, chips, chunk_rows, width), narrow),
             pltpu.VMEM((chunks, chips, chunk_rows, width), narrow),
@@ -446,9 +487,9 @@
             pltpu.VMEM((chunks, chunk_rows, other), wide),
             pltpu.VMEM((chunks, chunk_rows, half), wide),
             pltpu.VMEM((chunks, chunk_rows, width), narrow),
-            dma((1,)),
-            dma((3, devices)),
-            dma((3, devices)),
+            dma((2,)),
+            dma((2 + parts, devices)),
+            dma((2 + parts, devices)),
             dma((2, chunks)),
             dma((2, chunks)),
             dma((2, chunks)),
@@ -457,7 +498,7 @@
             dma((2, chunks)),
         ],
         compiler_params=pltpu.CompilerParams(
-            collective_id=0, has_side_effects=True, vmem_limit_bytes=48 * 1024 * 1024
+            collective_id=0, has_side_effects=True, vmem_limit_bytes=VMEM_GRANT
         ),
     )(gains, stream, queries[0], keys[0], values[0], out_weight[0])
     return out.reshape(1, rows, width)
@@ -483,7 +524,7 @@
     def step(stream, *rest):
         rows = stream.shape[0]
         if fits_by_head(mesh, rows):
-            return by_head(sections, CHUNKS, stream, *rest)
+            return by_head(sections, CHUNKS, PARTS, stream, *rest)
         return local(stream, *rest)
 
     return jax.shard_map(step, mesh=mesh, in_specs=in_specs, out_specs=out_specs, check_vma=False)

time: 71.6 us -> 61.2 us (0.85)
  Pallas kernels: 64.3 us -> 59.1 us
  local copies, waits for them, and re-layouts: 6.93 us -> 1.99 us
    pallas_call x1, Pallas kernels: 64.3 us -> 59.1 us  [by_head(): pl.pallas_call(functools.partial(fused_kernel, sections, chunks, parts, h...]
    unnamed x13 -> x1, local copies, waits for them, and re-layouts: 6.93 us -> 1.99 us
where the time goes in v2:
time: 61.2 us; the launch traced here: 61.1 us
  Pallas kernels  59.1 us (97%)
  local copies, waits for them, and re-layouts  1.99 us (3%)
    pallas_call x1, Pallas kernels, by_head(): pl.pallas_call(functools.partial(fused_kernel, sections, chunks, parts, h...  59.1 us
    unnamed x1, local copies, waits for them, and re-layouts  1.99 us

profile of v2, /device:TPU:24, one launch (start us, length us, event | category | flops | bytes accessed | tf_op | source)
XLA Modules:
  0.0 61.1 jit_solution(9657836449277208397)
XLA Ops:
  0.0 59.1 %shard_map.64 = bf16[8,16,2688]{2,1,0:T(8,128)(2,1)} custom-call(bf16[1,2688]{1,0:T(2,128)(2,1)} %gains_hbm.1, bf16[128,2688]{1,0:T(8,128)(2,1)} %stream_ref.1, bf16[128,2048]{1,0:T(8,128)(2,1)} %bitcast.7, bf16[128,1024]{1,0:T(8,128)(2,1)} %bitcast.8, bf16[128,1024]{1,0:T(8,128)(2,1)} %bitcast.9, bf16[256,2688]{1,0:T(8,128)(2,1)} %bitcast.6), custom_call_target="tpu_custom_call" | custom-call | tf_op jit(solution)/shard_map/pallas_call | solution.py:464
  59.1 2.0 %copy.8 = bf16[1,128,2688]{2,1,0:T(8,128)(2,1)} copy(bf16[1,128,2688]{2,1,0:T(8,128)(2,1)} %bitcast.5) | data formatting | bytes 1376256

commit v3 on v2

--- a/solution.py
+++ b/solution.py
@@ -262,6 +262,8 @@
                 arrive(1, vbuf.at[pl.ds(block * rows, rows)], block)
 
             arrive(2 + part, qbuf.at[block, pl.ds(low, part_rows)], block)
+
+        for block in range(devices):
             reach = (block + 1) * rows
             asked = jnp.concatenate(
                 [

time: 61.2 us -> 59.5 us (0.972)
  Pallas kernels: 59.1 us -> 57.3 us
    pallas_call x1, Pallas kernels: 59.1 us -> 57.3 us  [by_head(): pl.pallas_call(functools.partial(fused_kernel, sections, chunks, parts, h...]
where the time goes in v3:
time: 59.5 us; the launch traced here: 59.4 us
  Pallas kernels  57.3 us (96%)
  local copies, waits for them, and re-layouts  1.99 us (3%)
    pallas_call x1, Pallas kernels, by_head(): pl.pallas_call(functools.partial(fused_kernel, sections, chunks, parts, h...  57.3 us
    unnamed x1, local copies, waits for them, and re-layouts  1.99 us

profile of v3, /device:TPU:24, one launch (start us, length us, event | category | flops | bytes accessed | tf_op | source)
XLA Modules:
  0.0 59.4 jit_solution(13408432500381966974)
XLA Ops:
  0.0 57.3 %shard_map.64 = bf16[8,16,2688]{2,1,0:T(8,128)(2,1)} custom-call(bf16[1,2688]{1,0:T(2,128)(2,1)} %gains_hbm.1, bf16[128,2688]{1,0:T(8,128)(2,1)} %stream_ref.1, bf16[128,2048]{1,0:T(8,128)(2,1)} %bitcast.7, bf16[128,1024]{1,0:T(8,128)(2,1)} %bitcast.8, bf16[128,1024]{1,0:T(8,128)(2,1)} %bitcast.9, bf16[256,2688]{1,0:T(8,128)(2,1)} %bitcast.6), custom_call_target="tpu_custom_call" | custom-call | tf_op jit(solution)/shard_map/pallas_call | solution.py:466
  57.4 2.0 %copy.8 = bf16[1,128,2688]{2,1,0:T(8,128)(2,1)} copy(bf16[1,128,2688]{2,1,0:T(8,128)(2,1)} %bitcast.5) | data formatting | bytes 1376256
